TPU v7x, 32 devices: a whole 2x2x4 slice. The times are simulated.
32 devices in a mesh: sample: 8 (over y, x, core), chan: 4 (over z).
Axes of the slice: x: 2, y: 2, z: 4, core: 2. Of those that a mesh axis runs over, the one named last changes fastest.
Arguments:
- snapshots: bfloat16 [8, 256, 512], P('sample', None, 'chan'), may hold values from -6 to 6
- first_weight: bfloat16 [256, 27, 256], P('chan'), may hold values from -0.078125 to 0.078125
- second_weight: bfloat16 [256, 27, 256], P('chan'), may hold values from -0.078125 to 0.078125
- cotangent: bfloat16 [8, 256, 512], P('sample', 'chan'), may hold values from -0.09375 to 0.09375
Outputs:
- second_out: bfloat16 [8, 256, 512], P('sample', 'chan')
- first_grad: float32 [256, 27, 256], P('chan', None, 'sample')
- second_grad: float32 [256, 27, 256], P('chan', None, 'sample')
All inputs are finite; a program needn't handle non-finite values.
Results may differ from a plain program's by a relative error of at most 0.0061.
Values may be sent and summed in bfloat16 or wider, within the bound.
No kernel may reach another device: no remote copies, remote signals or barrier semaphores. Data moves between devices by JAX's collectives and lax.ppermute only.
A program may use at most 128 MiB of HBM per device.

v0:
```python
import jax
import jax.numpy as jnp
from jax import lax
from jax.sharding import PartitionSpec as P

SIDE = 8


def shifted(fields):
    batch_size, channels = (fields.shape[0], fields.shape[1])
    cube_form = fields.reshape(batch_size, channels, SIDE, SIDE, SIDE)
    padded = jnp.pad(cube_form, ((0, 0), (0, 0), (1, 1), (1, 1), (1, 1)))
    shifted_views = []
    for tap_index in range(27):
        shift_depth, shift_rows, shift_cols = (tap_index // 9, tap_index // 3 % 3, tap_index % 3)
        shifted_views.append(
            padded[
                :,
                :,
                shift_depth : shift_depth + SIDE,
                shift_rows : shift_rows + SIDE,
                shift_cols : shift_cols + SIDE,
            ]
        )
    return jnp.stack(shifted_views, axis=2).reshape(batch_size, channels * 27, SIDE * SIDE * SIDE)


def spread(terms):
    batch_size, channels = (terms.shape[0], terms.shape[1] // 27)
    cube_form = terms.reshape(batch_size, channels, 27, SIDE, SIDE, SIDE)
    padded = jnp.pad(cube_form, ((0, 0), (0, 0), (0, 0), (1, 1), (1, 1), (1, 1)))
    total = jnp.zeros((batch_size, channels, SIDE, SIDE, SIDE), jnp.float32)
    for tap_index in range(27):
        shift_depth, shift_rows, shift_cols = (tap_index // 9, tap_index // 3 % 3, tap_index % 3)
        total = (
            total
            + padded[
                :,
                :,
                tap_index,
                2 - shift_depth : 2 - shift_depth + SIDE,
                2 - shift_rows : 2 - shift_rows + SIDE,
                2 - shift_cols : 2 - shift_cols + SIDE,
            ]
        )
    return total.reshape(batch_size, channels, SIDE * SIDE * SIDE)


def layer_sums(kernel_rows, patches):
    partial_value = jnp.einsum(
        "kc,bkp->bcp", kernel_rows, patches, preferred_element_type=jnp.float32
    )
    return lax.psum_scatter(partial_value, "chan", scatter_dimension=1, tiled=True)


def all_channels(grad_maps):
    return lax.all_gather(grad_maps, "chan", axis=1, tiled=True)


def body(snapshots, first_weight, second_weight, cotangent):
    channel_maps = lax.all_to_all(snapshots, "chan", split_axis=1, concat_axis=2, tiled=True)
    input_patches = shifted(channel_maps)
    first_rows = first_weight.reshape(-1, first_weight.shape[2])
    second_rows = second_weight.reshape(-1, second_weight.shape[2])
    first_sum = layer_sums(first_rows, input_patches)
    first_map = first_sum.astype(jnp.bfloat16)
    first_values = first_map.astype(jnp.float32)
    hidden = jax.nn.silu(first_values).astype(jnp.bfloat16)
    hidden_patches = shifted(hidden)
    second_out = layer_sums(second_rows, hidden_patches).astype(jnp.bfloat16)
    full_cotangent = all_channels(cotangent)
    second_term = jnp.einsum(
        "bkp,bcp->kc", hidden_patches, full_cotangent, preferred_element_type=jnp.float32
    )
    terms = jnp.einsum(
        "kc,bcp->bkp", second_rows, full_cotangent, preferred_element_type=jnp.float32
    )
    hidden_grad = spread(terms)
    sigmoid_values = jax.nn.sigmoid(first_values)
    first_map_grad = (
        hidden_grad * sigmoid_values * (1.0 + first_values * (1.0 - sigmoid_values))
    ).astype(jnp.bfloat16)
    full_map_grad = all_channels(first_map_grad)
    first_term = jnp.einsum(
        "bkp,bcp->kc", input_patches, full_map_grad, preferred_element_type=jnp.float32
    )
    first_grad, second_grad = (
        lax.psum_scatter(first_term, "sample", scatter_dimension=1, tiled=True),
        lax.psum_scatter(second_term, "sample", scatter_dimension=1, tiled=True),
    )
    return (
        second_out,
        first_grad.reshape(first_weight.shape[0], 27, -1),
        second_grad.reshape(second_weight.shape[0], 27, -1),
    )


def solution(mesh):
    placed = (
        P("sample", None, "chan"),
        P("chan", None, None),
        P("chan", None, None),
        P("sample", "chan", None),
    )
    return jax.shard_map(
        body,
        mesh=mesh,
        in_specs=placed,
        out_specs=(P("sample", "chan", None), P("chan", None, "sample"), P("chan", None, "sample")),
        check_vma=False,
    )
```

profile of v0, /device:TPU:0, one launch (start us, length us, event | category | flops | bytes accessed | tf_op | source)
XLA Modules:
  0.0 640.3 jit_solution(11114681304338015524)
XLA Ops:
  7.2 1.0 copy.72
  8.7 1.0 reduce.22
  10.3 6.3 all-to-all-start
  16.7 1.7 copy.63
  18.3 1.2 reshape.411
  19.5 14.5 %all_gather.6 = bf16[1,256,512]{2,1,0:T(8,128)(2,1)S(1)} all-gather(bf16[1,64,512]{2,1,0:T(8,128)(2,1)S(1)} %copy-done.4), channel_id=1, replica_groups=mesh['sample'=8,'chan'=4] {'chan'}, dimensions={1}, use_global_device_ids=true | all-gather | bytes 327680 | tf_op jit(solution)/shard_map/all_gather | solution.py:57
  34.0 0.7 copy-done.1
  34.7 1.8 convolution_bitcast_fusion
  36.5 3.1 copy.65
  39.6 22.4 %reshape.413 = f32[1,64,27,8,8,8]{2,1,5,4,3,0:T(8,128)} reshape(f32[1,1728,512]{1,2,0:T(8,128)} %copy.65) | data formatting | bytes 7077888 | tf_op jit(solution)/shard_map/reshape | solution.py:30
  62.0 178.1 %fusion.16 = (f32[64,8,8,8]{0,3,2,1:T(8,128)S(1)}, f32[64,8,8,8]{0,3,2,1:T(8,128)S(1)}, f32[64,8,8,8]{0,3,2,1:T(8,128)S(1)}, f32[64,8,8,8]{0,3,2,1:T(8,128)S(1)}...) fusion(f32[1,64,27,8,8,8]{2,1,5,4,3,0:T(8,128)} %reshape.413), kind=kLoop, calls=%fused_computation.42 | loop fusion | flops 524288 | bytes 34996224 | tf_op jit(solution)/shard_map/slice | solution.py:37
  240.6 1.2 reshape.408
  243.1 0.9 reshape.443
  244.1 0.7 fusion.40
  247.5 0.7 fusion.50
  248.2 0.7 fusion.52
  251.6 0.7 fusion.62
  253.7 0.7 fusion.66
  254.4 0.7 fusion.68
  255.7 0.7 fusion.72
  257.8 0.7 fusion.78
  258.5 0.7 fusion.80
  262.6 9.5 %copy.58 = bf16[1,64,27,8,8,8]{2,1,5,4,3,0:T(8,128)(2,1)} copy(bf16[1,64,27,8,8,8]{1,5,4,3,2,0:T(8,128)(2,1)} %fusion.90) | data formatting | bytes 3538944 | tf_op jit(solution)/shard_map/stack | solution.py:25
  272.1 11.3 %reshape.407 = bf16[1728,512]{0,1:T(8,128)(2,1)S(1)} reshape(bf16[1,64,27,8,8,8]{2,1,5,4,3,0:T(8,128)(2,1)} %copy.58) | data formatting | bytes 3538944 | tf_op jit(solution)/shard_map/reshape.2
  283.4 2.6 convolution_bitcast_fusion.2
  286.0 1.3 copy.60
  287.3 140.8 %all-reduce.7 = bf16[1,256,512]{2,0,1:T(2,128)(2,1)} all-reduce(f32[1,256,512]{2,0,1:T(1,128)S(1)} %copy.60), channel_id=2, replica_groups=mesh['sample'=8,'chan'=4] {'chan'}, use_global_device_ids=true, to_apply=%region_0.1.clone | all-reduce | flops 131072 | bytes 786432
  428.1 1.0 constant_dynamic-slice_fusion
  429.3 1.6 fusion.33
  430.9 0.7 fusion.92
  434.3 0.7 fusion.102
  435.1 14.1 %all_gather.7 = bf16[1,256,512]{2,1,0:T(8,128)(2,1)S(1)} all-gather(bf16[1,64,512]{2,1,0:T(8,128)(2,1)S(1)} %copy.66), channel_id=1, replica_groups=mesh['sample'=8,'chan'=4] {'chan'}, dimensions={1}, use_global_device_ids=true | all-gather | bytes 327680 | tf_op jit(solution)/shard_map/all_gather | solution.py:57
  449.2 2.0 fusion.34
  451.3 0.7 fusion.104
  454.7 0.7 fusion.114
  456.8 0.7 fusion.118
  457.4 0.7 fusion.120
  458.8 0.7 fusion.124
  460.9 0.7 fusion.130
  461.6 0.7 fusion.132
  465.7 9.6 %copy.62 = bf16[1,64,27,8,8,8]{2,1,5,4,3,0:T(8,128)(2,1)} copy(bf16[1,64,27,8,8,8]{1,5,4,3,2,0:T(8,128)(2,1)} %fusion.142) | data formatting | bytes 3538944 | tf_op jit(solution)/shard_map/stack | solution.py:25
  475.2 11.3 %reshape.410 = bf16[1728,512]{0,1:T(8,128)(2,1)S(1)} reshape(bf16[1,64,27,8,8,8]{2,1,5,4,3,0:T(8,128)(2,1)} %copy.62) | data formatting | bytes 3538944 | tf_op jit(solution)/shard_map/reshape.5
  486.6 1.9 fusion.37
  489.6 136.3 %all-reduce.8 = bf16[1,256,512]{2,0,1:T(2,128)(2,1)S(1)} all-reduce(f32[1,256,512]{2,0,1:T(1,128)S(1)} %copy.64), channel_id=3, replica_groups=mesh['sample'=8,'chan'=4] {'chan'}, use_global_device_ids=true, to_apply=%region_1.2.clone | all-reduce | flops 131072 | bytes 786432
  626.7 2.2 reshape.415
  628.9 1.2 copy.68
  630.1 2.2 reshape.416
  632.3 1.2 copy.69
  (66 shorter events, 28.9 us)
Async XLA Ops:
  7.2 12.4 %copy-start.4 = (bf16[1,64,512]{2,1,0:T(8,128)(2,1)S(1)}, bf16[1,64,512]{2,1,0:T(8,128)(2,1)}, u32[]{:S(2)}) copy-start(bf16[1,64,512]{2,1,0:T(8,128)(2,1)} %param.7) | copy-start | bytes 196612
  10.3 232.7 %all-to-all-start = ((bf16[4,2,4096]{2,1,0:T(2,128)(2,1)}), bf16[4,2,4096]{2,1,0:T(2,128)(2,1)}, u32[]{:S(2)}, u32[]{:S(2)}) async-start(bf16[4,2,4096]{2,1,0:T(2,128)(2,1)} %reshape.442), calls=%async_computation | async-start | bytes 131072 | tf_op jit(solution)/shard_map/all_to_all | solution.py:61
  16.6 610.1 %reduce-scatter.3.cloned.1.call-start = ((), (), s32[]{:S(2)}) async-start(), calls=%async_computation.3 | async-start | bytes 2064384 | tf_op jit(solution)/shard_map/reduce_scatter | solution.py:88
  34.0 0.7 copy-start.1
  62.0 178.1 %copy-start.3 = (bf16[64,27,256]{2,0,1:T(8,128)(2,1)S(1)}, bf16[64,27,256]{2,0,1:T(8,128)(2,1)}, u32[]{:S(2)}) copy-start(bf16[64,27,256]{2,0,1:T(8,128)(2,1)} %param.5) | copy-start | bytes 2654212
  240.1 1.7 copy-start.5
  451.2 178.8 %reduce-scatter.5.cloned.1.call-start = ((), (), s32[]{:S(2)}) async-start(), calls=%async_computation.4 | async-start | bytes 2064384 | tf_op jit(solution)/shard_map/reduce_scatter | solution.py:89
  475.2 11.4 %copy-start.2 = (bf16[1,256,512]{2,1,0:T(8,128)(2,1)S(1)}, bf16[1,256,512]{2,1,0:T(8,128)(2,1)}, u32[]{:S(2)}) copy-start(bf16[1,256,512]{2,1,0:T(8,128)(2,1)} %copy-done.1) | copy-start | bytes 786436
  486.6 1.9 copy-start
Sparse Core Ops, SparseCore 0:
  451.4 40.2 reduce-scatter.2
  495.0 39.6 reduce-scatter.4
where the time goes:
time: 642 us; the launch traced here: 640 us
  blocking collectives  306 us (48%)
  other arithmetic  181 us (28%)
  local copies, waits for them, and re-layouts  124 us (19%)
  between operations  14.9 us (2%)
  matrix products  8.92 us (1%)
    unnamed x2, blocking collectives  277 us
    slice x1, other arithmetic, spread(): padded[:, :, tap_index, 2 - shift_depth:2 - shift_depth + SIDE, 2 - shift...  178 us
    unnamed x76, local copies, waits for them, and re-layouts  46.2 us
    all_gather x2, blocking collectives, all_channels(): return lax.all_gather(grad_maps, 'chan', axis=1, tiled=True)  28.6 us
    another operation x2, local copies, waits for them, and re-layouts  22.6 us
    reshape x1, local copies, waits for them, and re-layouts, spread(): cube_form = terms.reshape(batch_size, channels, 27, SIDE, SIDE, SIDE)  22.4 us
    another operation x4, local copies, waits for them, and re-layouts, shifted(): jnp.stack(shifted_views, axis=2)  20.4 us
  transfers between devices with their start and end apart: 3, of which 0 were waited for; matrix products, arithmetic and copies ran while one was open for 39% of the time, Pallas kernels for 0%

commit v1 on v0

--- a/solution.py
+++ b/solution.py
@@ -4,6 +4,18 @@
 from jax.sharding import PartitionSpec as P
 
 SIDE = 8
+
+
+def gather_by_bits(x, axis, dim):
+    ways, here, step = (lax.axis_size(axis), lax.axis_index(axis), x.shape[dim])
+    line, have = (x, 1)
+    while have < ways:
+        line = jnp.concatenate(
+            [line, lax.ppermute(line, axis, [(d, (d - have) % ways) for d in range(ways)])],
+            axis=dim,
+        )
+        have = 2 * have
+    return jnp.roll(line, here * step, axis=dim)
 
 
 def shifted(fields):
@@ -54,7 +66,7 @@
 
 
 def all_channels(grad_maps):
-    return lax.all_gather(grad_maps, "chan", axis=1, tiled=True)
+    return gather_by_bits(grad_maps, "chan", 1)
 
 
 def body(snapshots, first_weight, second_weight, cotangent):

time: 642 us -> 613 us (0.955)
  blocking collectives: 306 us -> 281 us
  local copies, waits for them, and re-layouts: 124 us -> 103 us
  waiting for transfers between devices: 0.04 us -> 11.2 us
  starting transfers between devices: 6.36 us -> 13.1 us
    all_gather x2 -> x0, blocking collectives: 28.6 us -> none  [all_channels(): return lax.all_gather(grad_maps, 'chan', axis=1, tiled=True)]
    unnamed x76 -> x82, local copies, waits for them, and re-layouts: 46.2 us -> 29.2 us
    ppermute x0 -> x4, waiting for transfers between devices: none -> 11.1 us  [gather_by_bits(): lax.ppermute(line, axis, [(d, (d - have) % ways) for d in range(ways)])]
    ppermute x0 -> x4, starting transfers between devices: none -> 9.73 us  [gather_by_bits(): lax.ppermute(line, axis, [(d, (d - have) % ways) for d in range(ways)])]
  transfers between devices with their start and end apart: 3 -> 7, of which waited for: 0 -> 2; matrix products, arithmetic and copies ran while one was open for 39% -> 10% of each run, Pallas kernels for 0% -> 0%
where the time goes in v1:
time: 613 us; the launch traced here: 612 us
  blocking collectives  281 us (46%)
  other arithmetic  180 us (29%)
  local copies, waits for them, and re-layouts  103 us (17%)
  between operations  15.1 us (2%)
  starting transfers between devices  13.1 us (2%)
  waiting for transfers between devices  11.2 us (2%)
  matrix products  8.82 us (1%)
    unnamed x2, blocking collectives  281 us
    slice x1, other arithmetic, spread(): padded[:, :, tap_index, 2 - shift_depth:2 - shift_depth + SIDE, 2 - shift...  177 us
    unnamed x82, local copies, waits for them, and re-layouts  29.2 us
    another operation x2, local copies, waits for them, and re-layouts  22.6 us
    reshape x1, local copies, waits for them, and re-layouts, spread(): cube_form = terms.reshape(batch_size, channels, 27, SIDE, SIDE, SIDE)  22.4 us
    another operation x4, local copies, waits for them, and re-layouts, shifted(): jnp.stack(shifted_views, axis=2)  17.8 us
  transfers between devices with their start and end apart: 7, of which 2 were waited for; matrix products, arithmetic and copies ran while one was open for 10% of the time, Pallas kernels for 0%

profile of v1, /device:TPU:0, one launch (start us, length us, event | category | flops | bytes accessed | tf_op | source)
XLA Modules:
  0.0 612.1 jit_solution(15824838282711595184)
XLA Ops:
  7.2 5.1 collective-permute-start
  12.3 0.9 copy.71
  13.7 1.0 reduce.22
  15.4 3.3 all-to-all-start
  18.8 1.7 copy.63
  20.5 1.2 reshape.411
  24.5 2.8 collective-permute-start.1
  27.5 0.7 fusion.50
  28.9 0.7 fusion.54
  30.9 0.7 fusion.60
  31.6 0.7 fusion.62
  33.0 0.7 fusion.66
  33.7 0.7 fusion.68
  35.0 0.7 fusion.72
  35.7 0.7 fusion.74
  37.1 0.7 fusion.76
  37.8 0.7 fusion.78
  39.1 0.7 fusion.82
  39.8 0.7 fusion.84
  41.2 0.7 fusion.88
  41.9 0.7 fusion.90
  43.9 0.7 fusion.96
  45.3 0.7 fusion.100
  46.0 9.5 %copy.58 = bf16[1,64,27,8,8,8]{2,1,5,4,3,0:T(8,128)(2,1)} copy(bf16[1,64,27,8,8,8]{1,5,4,3,2,0:T(8,128)(2,1)} %fusion.100) | data formatting | bytes 3538944 | tf_op jit(solution)/shard_map/stack | solution.py:37
  55.5 11.3 %reshape.407 = bf16[1728,512]{0,1:T(8,128)(2,1)S(1)} reshape(bf16[1,64,27,8,8,8]{2,1,5,4,3,0:T(8,128)(2,1)} %copy.58) | data formatting | bytes 3538944 | tf_op jit(solution)/shard_map/reshape.2
  66.8 1.2 copy-done.3
  69.1 143.3 %all-reduce.7 = bf16[1,256,512]{2,0,1:T(2,128)(2,1)S(1)} all-reduce(f32[1,256,512]{2,0,1:T(1,128)S(1)} %copy.60), channel_id=2, replica_groups=mesh['sample'=8,'chan'=4] {'chan'}, use_global_device_ids=true, to_apply=%region_0.1.clone | all-reduce | flops 131072 | bytes 786432
  212.5 0.8 copy.61
  213.3 1.0 fusion.46
  214.3 0.7 copy-done.1
  215.0 1.8 convolution_bitcast_fusion
  216.7 3.1 copy.65
  219.9 22.4 %reshape.413 = f32[1,64,27,8,8,8]{2,1,5,4,3,0:T(8,128)} reshape(f32[1,1728,512]{1,2,0:T(8,128)} %copy.65) | data formatting | bytes 7077888 | tf_op jit(solution)/shard_map/reshape | solution.py:42
  242.3 176.8 %fusion.16 = (f32[64,8,8,8]{0,3,2,1:T(8,128)S(1)}, f32[64,8,8,8]{0,3,2,1:T(8,128)S(1)}, f32[64,8,8,8]{0,3,2,1:T(8,128)S(1)}, f32[64,8,8,8]{0,3,2,1:T(8,128)S(1)}...) fusion(f32[1,64,27,8,8,8]{2,1,5,4,3,0:T(8,128)} %reshape.413), kind=kLoop, calls=%fused_computation.42 | loop fusion | flops 524288 | bytes 34996224 | tf_op jit(solution)/shard_map/slice | solution.py:49
  419.1 0.9 fusion.33
  421.4 7.6 %copy.62 = bf16[1,64,27,8,8,8]{2,1,5,4,3,0:T(8,128)(2,1)} copy(bf16[1,64,27,8,8,8]{1,5,4,3,2,0:T(8,128)(2,1)S(1)} %fusion.152) | data formatting | bytes 3538944 | tf_op jit(solution)/shard_map/stack | solution.py:37
  429.0 11.3 %reshape.410 = bf16[1728,512]{0,1:T(8,128)(2,1)S(1)} reshape(bf16[1,64,27,8,8,8]{2,1,5,4,3,0:T(8,128)(2,1)} %copy.62) | data formatting | bytes 3538944 | tf_op jit(solution)/shard_map/reshape.5
  440.3 1.9 fusion.155
  442.3 0.9 collective-permute-start.2
  443.2 5.4 collective-permute-done.2
  448.8 0.9 collective-permute-start.3
  449.7 5.7 collective-permute-done.3
  455.4 3.9 fusion.38
  460.3 137.4 %all-reduce.8 = bf16[1,256,512]{2,0,1:T(2,128)(2,1)S(1)} all-reduce(f32[1,256,512]{2,0,1:T(1,128)S(1)} %copy.64), channel_id=3, replica_groups=mesh['sample'=8,'chan'=4] {'chan'}, use_global_device_ids=true, to_apply=%region_1.2.clone | all-reduce | flops 131072 | bytes 786432
  598.5 2.2 reshape.416
  600.7 1.2 copy.68
  601.9 2.2 reshape.415
  604.1 1.2 copy.67
  (80 shorter events, 15.4 us)
Async XLA Ops:
  7.2 14.6 %copy-start.4 = (bf16[64,27,256]{2,0,1:T(8,128)(2,1)S(1)}, bf16[64,27,256]{2,0,1:T(8,128)(2,1)}, u32[]{:S(2)}) copy-start(bf16[64,27,256]{2,0,1:T(8,128)(2,1)} %param.7) | copy-start | bytes 2654212
  7.2 16.6 %collective-permute-start = (bf16[1,64,512]{2,1,0:T(8,128)(2,1)}, bf16[1,64,512]{2,1,0:T(8,128)(2,1)S(1)}, u32[]{:S(2)}, u32[]{:S(2)}) collective-permute-start(bf16[1,64,512]{2,1,0:T(8,128)(2,1)} %param.9), channel_id=1, source_target_pairs={{0,3},{1,0},{2,1},{3,2},{4,7},{5,4},{6,5},{7,6},{8,11},{9,8},{10,9... | collective-permute-start | bytes 196616 | tf_op jit(solution)/shard_map/ppermute | solution.py:14
  15.4 11.9 %all-to-all-start = ((bf16[4,2,4096]{2,1,0:T(2,128)(2,1)}), bf16[4,2,4096]{2,1,0:T(2,128)(2,1)S(1)}, u32[]{:S(2)}, u32[]{:S(2)}) async-start(bf16[4,2,4096]{2,1,0:T(2,128)(2,1)} %reshape.442), calls=%async_computation | async-start | bytes 131072 | tf_op jit(solution)/shard_map/all_to_all | solution.py:73
  18.7 579.8 %reduce-scatter.5.cloned.1.call-start = ((), (), s32[]{:S(2)}) async-start(), calls=%async_computation.4 | async-start | bytes 2064384 | tf_op jit(solution)/shard_map/reduce_scatter | solution.py:101
  18.8 3.8 copy-start.8
  18.8 5.0 copy-start.7
  24.5 188.8 %collective-permute-start.1 = (bf16[1,128,512]{2,1,0:T(8,128)(2,1)}, bf16[1,128,512]{2,1,0:T(8,128)(2,1)S(1)}, u32[]{:S(2)}, u32[]{:S(2)}) collective-permute-start(bf16[1,128,512]{2,1,0:T(8,128)(2,1)} %pad_maximum_fusion), channel_id=1, source_target_pairs={{0,2},{1,3},{2,0},{3,1},{4,6},{5,7},{6,4},{7,5},{8,10},{9,11},{10,... | collective-permute-start | bytes 393224 | tf_op jit(solution)/shard_map/ppermute | solution.py:14
  66.8 1.2 copy-start.3
  214.2 0.7 copy-start.1
  242.3 176.8 %copy-start.6 = (bf16[1,64,512]{1,2,0:T(8,128)(2,1)S(1)}, bf16[1,64,512]{1,2,0:T(8,128)(2,1)}, u32[]{:S(2)}) copy-start(bf16[1,64,512]{1,2,0:T(8,128)(2,1)} %copy.61) | copy-start | bytes 196612
  429.0 11.4 %copy-start.2 = (bf16[256,512]{1,0:T(8,128)(2,1)S(1)}, bf16[256,512]{1,0:T(8,128)(2,1)}, u32[]{:S(2)}) copy-start(bf16[256,512]{1,0:T(8,128)(2,1)} %copy-done.1) | copy-start | bytes 786436
  440.3 2.0 copy-start.5
  442.2 159.7 %reduce-scatter.3.cloned.1.call-start = ((), (), s32[]{:S(2)}) async-start(), calls=%async_computation.3 | async-start | bytes 2064384 | tf_op jit(solution)/shard_map/reduce_scatter | solution.py:100
  442.3 6.3 %collective-permute-start.2 = (bf16[1,64,512]{1,2,0:T(8,128)(2,1)S(1)}, bf16[1,64,512]{1,2,0:T(8,128)(2,1)S(1)}, u32[]{:S(2)}, u32[]{:S(2)}) collective-permute-start(bf16[1,64,512]{1,2,0:T(8,128)(2,1)S(1)} %copy-done.5), channel_id=1, source_target_pairs={{0,3},{1,0},{2,1},{3,2},{4,7},{5,4},{6,5},{7,6},{8,11},{9,8},{10,9... | collective-permute-start | bytes 196616 | tf_op jit(solution)/shard_map/ppermute | solution.py:14
  448.7 10.5 %copy-start = (bf16[1728,256]{1,0:T(8,128)(2,1)S(1)}, bf16[1728,256]{1,0:T(8,128)(2,1)}, u32[]{:S(2)}) copy-start(bf16[1728,256]{1,0:T(8,128)(2,1)} %reshape.411) | copy-start | bytes 2654212
  448.8 6.6 %collective-permute-start.3 = (bf16[1,128,512]{1,2,0:T(8,128)(2,1)S(1)}, bf16[1,128,512]{1,2,0:T(8,128)(2,1)S(1)}, u32[]{:S(2)}, u32[]{:S(2)}) collective-permute-start(bf16[1,128,512]{1,2,0:T(8,128)(2,1)S(1)} %pad_maximum_fusion.1), channel_id=1, source_target_pairs={{0,2},{1,3},{2,0},{3,1},{4,6},{5,7},{6,4},{7,5},{8,10},{9,11},{10,... | collective-permute-start | bytes 393224 | tf_op jit(solution)/shard_map/ppermute | solution.py:14
Sparse Core Ops, SparseCore 0:
  442.4 38.5 reduce-scatter.4
  484.3 39.6 reduce-scatter.2
